TPU v7x, 32 devices: a whole 2x2x4 slice. The times are simulated.
32 devices in a mesh: slab: 4 (over y, x), leaf: 8 (over z, core).
Axes of the slice: x: 2, y: 2, z: 4, core: 2. Of those that a mesh axis runs over, the one named last changes fastest.
Arguments:
- right_sides: bfloat16 [32, 131072], P(None, ('slab', 'leaf')), may hold values from -6 to 6
- left_sides: bfloat16 [32, 131072], P(None, ('slab', 'leaf')), may hold values from -6 to 6
- near_blocks: bfloat16 [1024, 8, 128, 128], P(('slab', 'leaf')), may hold values from -0.1875 to 0.1875
- near_columns: int32 [1024, 8], P(('slab', 'leaf')), may hold values from 0 to 1023, as said below
- cluster_points: int32 [1024], P(('slab', 'leaf')), may hold values from 64 to 128, as said below
- leaf_basis: bfloat16 [1024, 64, 128], P(('slab', 'leaf')), may hold values from -0.5 to 0.5
- transfer: float32 [1024, 64, 128], P(('slab', 'leaf')), may hold values from -0.625 to 0.625
- far_parents: int32 [32, 24], P(('slab', 'leaf')), may hold values from 0 to 31, as said below
- far_count: int32 [32], P(('slab', 'leaf')), may hold values from 12 to 24, as said below
- coupling: float32 [32, 24, 128, 128], P(('slab', 'leaf')), may hold values from -0.375 to 0.375
- slab_transfer: float32 [32, 128, 128], P(('slab', 'leaf')), may hold values from -0.75 to 0.75
- apex_coupling: float32 [4, 4, 128, 128], replicated, may hold values from -0.75 to 0.75
Outputs:
- product: float32 [32, 131072], P(None, ('slab', 'leaf'))
- adjoint_product: float32 [32, 131072], P(None, ('slab', 'leaf'))
Inputs may be any that keep to these rules, and one draw needn't show every extreme that they name: `near_columns`: row i holds 8 different clusters, i among them, all inside the window of 9 consecutive clusters centred on i, moved inward where it would pass an end of 0 to 1023. `cluster_points`: some cluster has exactly 128 points and some exactly 64. `far_parents`: row p holds 24 different parents, none equal to p; only the first far_count[p] are used. `far_count`: some parent uses all 24 slots and some exactly 12.
All inputs are finite; a program needn't handle non-finite values.
Results may differ from a plain program's by a relative error of at most 0.0024.
Values may be sent and summed in bfloat16 or wider, within the bound.
A program may use at most 128 MiB of HBM per device.

v0:
```python
import jax
import jax.numpy as jnp
from jax import lax
from jax.sharding import PartitionSpec as P

B = 128
HW = 4


def extended_2(value, sides, width):
    for axis, dim in sides:
        size, length = (lax.axis_size(axis), value.shape[dim])
        up = [(i, (i + 1) % size) for i in range(size - 1)]
        down = [(j, i) for i, j in up]
        last = lax.slice_in_dim(value, length - width, length, axis=dim)
        first = lax.slice_in_dim(value, 0, width, axis=dim)
        before = lax.ppermute(last, axis, up)
        after = lax.ppermute(first, axis, down)
        value = jnp.concatenate([before, value, after], axis=dim)
    return value


def passed_along(block, axis, distance):
    devices = range(lax.axis_size(axis))
    route = [(i - distance, i) for i in devices if i - distance in devices]
    return lax.ppermute(block, axis, route)


def shards(
    right_sides,
    left_sides,
    near_blocks,
    near_columns,
    cluster_points,
    leaf_basis,
    transfer,
    far_parents,
    far_count,
    coupling,
    slab_transfer,
    apex_coupling,
):
    uppermost_level = lax.Precision.HIGHEST
    rhs_count = right_sides.shape[0]
    clusters = near_blocks.shape[0]
    device = lax.axis_index(("slab", "leaf"))
    devices_all = lax.axis_size(("slab", "leaf"))
    slab_index = lax.axis_index("slab")
    slab_count = lax.axis_size("slab")
    point_mask = jnp.arange(B, dtype=jnp.int32)[None, :] < cluster_points[:, None]
    zero_bf = jnp.zeros((), jnp.bfloat16)
    masked_right = jnp.where(point_mask[None], right_sides.reshape(rhs_count, clusters, B), zero_bf)
    masked_left = jnp.where(point_mask[None], left_sides.reshape(rhs_count, clusters, B), zero_bf)
    extended = extended_2(
        masked_right.reshape(rhs_count, clusters * B), ((("slab", "leaf"), 1),), HW * B
    )
    extended = extended.reshape(rhs_count, clusters + 2 * HW, B)
    offsets = near_columns - (device * clusters - HW)
    picked = jnp.take(extended, offsets, axis=1)
    near_out = jnp.einsum("csab,rcsb->rca", near_blocks, picked, preferred_element_type=jnp.float32)
    contrib = jnp.einsum(
        "csab,rca->csrb", near_blocks, masked_left, preferred_element_type=jnp.float32
    )
    collected = jax.ops.segment_sum(
        contrib.reshape(-1, rhs_count, B), offsets.reshape(-1), num_segments=clusters + 2 * HW
    )
    from_next = passed_along(collected[:HW].astype(jnp.bfloat16), ("slab", "leaf"), -1).astype(
        jnp.float32
    )
    from_prev = passed_along(
        collected[clusters + HW :].astype(jnp.bfloat16), ("slab", "leaf"), 1
    ).astype(jnp.float32)
    middle = collected[HW : clusters + HW]
    middle = middle.at[clusters - HW :].add(from_next).at[:HW].add(from_prev)
    near_back = jnp.transpose(middle, (1, 0, 2))
    leaf_right = jnp.einsum(
        "ckb,rcb->ckr", leaf_basis, masked_right, preferred_element_type=jnp.float32
    )
    leaf_left = jnp.einsum(
        "ckb,rcb->ckr", leaf_basis, masked_left, preferred_element_type=jnp.float32
    )
    parent_right = jnp.einsum("ckq,ckr->qr", transfer, leaf_right, precision=uppermost_level)
    parent_left = jnp.einsum("ckq,ckr->qr", transfer, leaf_left, precision=uppermost_level)
    targets = far_parents[0]
    live_slots = jnp.arange(targets.shape[0], dtype=jnp.int32) < far_count[0]
    couple = coupling[0]
    piece = lax.all_gather(parent_right[None], ("slab", "leaf"), axis=0, tiled=True)
    owners = jnp.arange(piece.shape[0], dtype=jnp.int32)
    select = ((targets[:, None] == owners[None, :]) & live_slots[:, None]).astype(jnp.float32)
    chosen = jnp.einsum("fn,nqr->fqr", select, piece, precision=uppermost_level)
    far_right = jnp.einsum("fab,fbr->ar", couple, chosen, precision=uppermost_level)
    outward = jnp.einsum("fab,ar->fbr", couple, parent_left, precision=uppermost_level)
    routing = (
        (targets[:, None] == jnp.arange(devices_all, dtype=jnp.int32)[None, :])
        & live_slots[:, None]
    ).astype(jnp.float32)
    spread = jnp.einsum("fp,fbr->pbr", routing, outward, precision=uppermost_level)
    arrived = lax.all_to_all(spread, ("slab", "leaf"), split_axis=0, concat_axis=0, tiled=True)
    far_left = jnp.sum(arrived, axis=0)
    lift = slab_transfer[0]
    slab_share = jnp.stack(
        [
            jnp.einsum("qt,qr->tr", lift, parent_right, precision=uppermost_level),
            jnp.einsum("qt,qr->tr", lift, parent_left, precision=uppermost_level),
        ]
    )
    within = lax.psum(slab_share, "leaf")
    slab_sum_totals = lax.all_gather(within[None], "slab", axis=0, tiled=True)
    remaining_slabs = (jnp.arange(slab_count, dtype=jnp.int32) != slab_index).astype(jnp.float32)
    row_block_list = lax.dynamic_index_in_dim(apex_coupling, slab_index, 0, keepdims=False)
    column_blocks = lax.dynamic_index_in_dim(apex_coupling, slab_index, 1, keepdims=False)
    apex_right = jnp.einsum(
        "j,jiv,jvq->iq",
        remaining_slabs,
        row_block_list,
        slab_sum_totals[:, 0],
        precision=uppermost_level,
    )
    apex_left = jnp.einsum(
        "s,sab,sar->br",
        remaining_slabs,
        column_blocks,
        slab_sum_totals[:, 1],
        precision=uppermost_level,
    )
    hat_right = far_right + jnp.einsum("qt,tr->qr", lift, apex_right, precision=uppermost_level)
    hat_left = far_left + jnp.einsum("qt,tr->qr", lift, apex_left, precision=uppermost_level)
    down_right = jnp.einsum("ckq,qr->ckr", transfer, hat_right, precision=uppermost_level).astype(
        jnp.bfloat16
    )
    down_left = jnp.einsum("ckq,qr->ckr", transfer, hat_left, precision=uppermost_level).astype(
        jnp.bfloat16
    )
    far_out = jnp.einsum("ckb,ckr->rcb", leaf_basis, down_right, preferred_element_type=jnp.float32)
    far_back = jnp.einsum("ckb,ckr->rcb", leaf_basis, down_left, preferred_element_type=jnp.float32)
    zero_wide = jnp.zeros((), jnp.float32)
    product = jnp.where(point_mask[None], near_out + far_out, zero_wide).reshape(
        rhs_count, clusters * B
    )
    adjoint_product = jnp.where(point_mask[None], near_back + far_back, zero_wide).reshape(
        rhs_count, clusters * B
    )
    return (product, adjoint_product)


def solution(mesh):
    return jax.shard_map(
        shards,
        mesh=mesh,
        in_specs=(
            P(None, ("slab", "leaf")),
            P(None, ("slab", "leaf")),
            P(("slab", "leaf"), None, None, None),
            P(("slab", "leaf"), None),
            P(("slab", "leaf")),
            P(("slab", "leaf"), None, None),
            P(("slab", "leaf"), None, None),
            P(("slab", "leaf"), None),
            P(("slab", "leaf")),
            P(("slab", "leaf"), None, None, None),
            P(("slab", "leaf"), None, None),
            P(),
        ),
        out_specs=(P(None, ("slab", "leaf")), P(None, ("slab", "leaf"))),
        check_vma=False,
    )
```

profile of v0, /device:TPU:0, one launch (start us, length us, event | category | flops | bytes accessed | tf_op | source)
XLA Modules:
  0.0 178.2 jit_solution(13958339036343607816)
XLA Ops:
  0.6 0.0 copy-start
  0.7 0.8 compare_and_fusion
  1.5 0.1 copy.46
  1.5 0.1 reshape.132
  1.6 0.7 iota_compare_fusion
  2.4 6.7 %fusion.31 = f32[32,32,8,128]{3,1,2,0:T(8,128)} fusion(bf16[32,8,128,128]{3,2,1,0:T(8,128)(2,1)} %param.18, pred[32,128]{1,0:T(8,128)(4,1)S(1)} %iota_compare_fusion, bf16[32,4096]{1,0:T(8,128)(2,1)} %param.17), kind=kOutput, calls=%fused_computation.45 | convolution fusion | flops 268566528 | bytes 12849152 | tf_op jit(solution)/shard_map/csab,rca->csrb/dot_general | solution.py:61
  9.0 0.1 broadcast_in_dim.78
  9.1 0.0 copy-start.4
  9.1 22.6 %scatter_fusion = f32[40,32,128]{2,1,0:T(8,128)S(1)} fusion(f32[40,32,128]{2,1,0:T(8,128)S(1)} %broadcast_in_dim.78, s32[256]{0:T(256)S(1)} %reshape.132, f32[256,32,128]{2,1,0:T(8,128)} %bitcast.168), kind=kCustom, calls=%fused_computation.1 | custom fusion | flops 1048576 | bytes 12583936 | tf_op jit(solution)/shard_map/scatter-add | solution.py:64
  31.7 0.0 copy-start.1
  31.7 0.1 convert.9
  31.8 0.6 fusion.70
  32.4 1.3 collective-permute-start.2
  33.7 3.7 %collective-permute-start.3 = (bf16[4,32,128]{2,1,0:T(8,128)(2,1)}, bf16[4,32,128]{2,1,0:T(8,128)(2,1)}, u32[]{:S(2)}, u32[]{:S(2)}) collective-permute-start(bf16[4,32,128]{2,1,0:T(8,128)(2,1)} %get-tuple-element.28), channel_id=1, source_target_pairs={{0,1},{1,2},{2,3},{3,4},{4,5},{5,6},{6,7},{7,8},{8,9},{9,10},{10,1... | collective-permute-start | bytes 98312 | tf_op jit(solution)/shard_map/ppermute | solution.py:26
  37.4 1.4 convolution_bitcast_fusion
  39.5 0.7 fusion.73
  40.2 0.0 copy-start.8
  40.3 0.0 copy-start.13
  40.3 0.9 fusion.15
  41.2 0.6 fusion.27
  41.9 1.1 copy.48
  43.0 10.2 %all-to-all-start = ((f32[32,128,32]{1,2,0:T(8,128)}), f32[32,128,32]{1,2,0:T(8,128)}, u32[]{:S(2)}, u32[]{:S(2)}) async-start(f32[32,128,32]{1,2,0:T(8,128)} %copy.48), calls=%async_computation | async-start | bytes 1048576 | tf_op jit(solution)/shard_map/all_to_all | solution.py:98
  53.2 0.1 lt.59
  53.3 1.0 broadcast_select_fusion
  54.3 0.6 fusion.71
  54.9 2.7 %collective-permute-start = (bf16[32,512]{1,0:T(8,128)(2,1)}, bf16[32,512]{1,0:T(8,128)(2,1)}, u32[]{:S(2)}, u32[]{:S(2)}) collective-permute-start(bf16[32,512]{1,0:T(8,128)(2,1)} %get-tuple-element.30), channel_id=1, source_target_pairs={{0,1},{1,2},{2,3},{3,4},{4,5},{5,6},{6,7},{7,8},{8,9},{9,10},{10,1... | collective-permute-start | bytes 98312 | tf_op jit(solution)/shard_map/ppermute | solution.py:17
  57.6 1.3 collective-permute-start.1
  58.9 2.3 %convolution_bitcast_fusion.1 = f32[32,64,32]{1,2,0:T(8,128)} fusion(bf16[32,64,128]{2,1,0:T(8,128)(2,1)} %param.21, pred[32,128]{1,0:T(8,128)(4,1)S(1)} %iota_compare_fusion, bf16[32,4096]{1,0:T(8,128)(2,1)} %param.16), kind=kOutput, calls=%fused_computation.12 | convolution fusion | flops 16908288 | bytes 1052672 | tf_op jit(solution)/shard_map/ckb,rcb->ckr/dot_general | solution.py:76
  61.2 1.0 convolution_bitcast_fusion.5
  62.2 1.8 %fusion.72 = f32[32,128,1]{1,0,2:T(8,128)S(1)} fusion(f32[32,64,32]{1,2,0:T(8,128)} %convolution_bitcast_fusion.1, f32[32,64,128]{2,1,0:T(8,128)S(1)} %copy-done.1), kind=kOutput, calls=%fused_computation.97 | convolution fusion | flops 100663296 | bytes 1327104 | tf_op jit(solution)/shard_map/ckq,ckr->qr/dot_general | solution.py:82
  64.0 0.0 copy-start.9
  64.0 0.6 copy-done.9
  64.6 1.0 convolution_bitcast_fusion.6
  65.6 0.6 maximum_bitcast_fusion.1
  66.2 31.6 %psum.7 = f32[1,2,128,32]{2,3,1,0:T(8,128)} all-reduce(f32[1,2,128,32]{2,3,1,0:T(8,128)} %maximum_bitcast_fusion.1), channel_id=1, replica_groups=mesh['slab'=4,'leaf'=8] {'leaf'}, use_global_device_ids=true, to_apply=%region_0.1 | all-reduce | flops 8192 | bytes 65536 | tf_op jit(solution)/shard_map/psum | solution.py:107
  97.8 10.0 %all_gather.7 = f32[4,2,128,32]{2,3,1,0:T(8,128)} all-gather(f32[1,2,128,32]{2,3,1,0:T(8,128)} %psum.7), channel_id=1, replica_groups=mesh['slab'=4,'leaf'=8] {'slab'}, dimensions={0}, use_global_device_ids=true | all-gather | bytes 163840 | tf_op jit(solution)/shard_map/all_gather | solution.py:108
  107.8 1.8 %convolution_bitcast_fusion.3 = f32[128,32]{0,1:T(8,128)} fusion(f32[4,4,128,128]{3,2,1,0:T(8,128)} %param.27, s32[]{:T(128)S(6)} %select_n.42, f32[4,2,128,32]{2,3,1,0:T(8,128)} %all_gather.7, f32[4]{0:T(128)S(1)} %compare_convert_fusion), kind=kOutput, calls=%fused_computation.28 | convolution fusion | flops 25182208 | bytes 344084 | tf_op jit(solution)/shard_map/s,sab,sar->br/dot_general | solution.py:119
  109.6 1.4 convolution_bitcast_fusion.4
  111.0 39.0 %all-gather = f32[4096,32]{0,1:T(8,128)S(1)} all-gather(f32[128,32]{0,1:T(8,128)} %bitcast.174), channel_id=2, replica_groups=mesh['slab'=4,'leaf'=8] {'slab','leaf'}, dimensions={0}, use_global_device_ids=true | all-gather | bytes 540672 | tf_op jit(solution)/shard_map/all_gather | solution.py:87
  150.0 0.1 copy.58
  150.1 1.0 fusion.58
  151.2 1.6 fusion.20
  152.8 0.2 fusion.25
  153.0 3.6 %fusion.18 = bf16[32,64,32]{1,2,0:T(8,128)(2,1)} fusion(f32[32,128,1]{1,0,2:T(8,128)S(1)} %fusion.25, f32[32,64,128]{2,1,0:T(8,128)S(1)} %copy-done.1), kind=kOutput, calls=%fused_computation.22 | convolution fusion | flops 100728832 | bytes 1196032 | tf_op jit(solution)/shard_map/ckq,qr->ckr/dot_general | solution.py:128
  156.6 0.1 copy.39
  156.7 0.1 reshape.124
  156.8 0.8 slice.86
  157.6 0.1 copy.38
  157.7 0.8 copy_bitcast_fusion.2
  158.6 2.2 %gather_fusion = bf16[256,32,128]{2,1,0:T(8,128)(2,1)} fusion(bf16[32,40,128]{2,0,1:T(8,128)(2,1)S(1)} %copy_bitcast_fusion.2, s32[1024]{0:T(1024)S(1)} %pad_clamp_fusion), kind=kCustom, calls=%fused_computation | custom fusion | bytes 4195328 | tf_op jit(solution)/shard_map/jit(_take)/gather | solution.py:59
  160.8 1.4 fusion.44
  162.2 6.9 %fusion.8 = f32[32,32,128]{2,1,0:T(8,128)S(1)} fusion(bf16[32,8,128,128]{3,2,1,0:T(8,128)(2,1)} %param.18, bf16[32,8,32,128]{3,2,1,0:T(8,128)(2,1)} %bitcast.169, pred[32,8]{1,0:T(8,128)(4,1)S(1)} %copy.38), kind=kOutput, calls=%fused_computation.10 | convolution fusion | flops 269484032 | bytes 11010304 | tf_op jit(solution)/shard_map/csab,rcsb->rca/dot_general | solution.py:60
  169.1 0.0 copy-done.3
  169.2 0.0 copy-start.6
  169.2 0.0 copy-start.2
  169.2 0.3 fusion.14
  169.5 0.8 copy.76
  170.3 1.5 fusion.43
  171.8 1.1 reduce_sum.9
  172.9 0.2 fusion.24
  173.1 0.0 copy-done.2
  173.1 2.9 %fusion.19 = bf16[32,64,32]{1,2,0:T(8,128)(2,1)S(1)} fusion(f32[128,32,1]{0,1,2:T(8,128)S(1)} %fusion.24, f32[32,64,128]{2,1,0:T(8,128)S(1)} %copy-done.2), kind=kOutput, calls=%fused_computation.23 | convolution fusion | flops 100728832 | bytes 1196032 | tf_op jit(solution)/shard_map/ckq,qr->ckr/dot_general | solution.py:131
  176.0 1.3 fusion.12
  177.4 0.8 copy.75
  (27 shorter events, 0.1 us)
Async XLA Ops:
  0.6 39.6 %copy-start = (f32[1,24,128,128]{3,2,1,0:T(8,128)S(1)}, f32[1,24,128,128]{3,2,1,0:T(8,128)}, u32[]{:S(2)}) copy-start(f32[1,24,128,128]{3,2,1,0:T(8,128)} %param.25) | copy-start | bytes 4718596
  9.1 28.3 %copy-start.4 = (bf16[32,4096]{1,0:T(8,128)(2,1)S(1)}, bf16[32,4096]{1,0:T(8,128)(2,1)}, u32[]{:S(2)}) copy-start(bf16[32,4096]{1,0:T(8,128)(2,1)} %param.17) | copy-start | bytes 786436
  31.7 7.8 %copy-start.1 = (f32[32,64,128]{2,1,0:T(8,128)S(1)}, f32[32,64,128]{2,1,0:T(8,128)}, u32[]{:S(2)}) copy-start(f32[32,64,128]{2,1,0:T(8,128)} %param.22) | copy-start | bytes 3145732
  32.4 128.4 %collective-permute-start.2 = (bf16[4,32,128]{2,1,0:T(8,128)(2,1)}, bf16[4,32,128]{2,1,0:T(8,128)(2,1)}, u32[]{:S(2)}, u32[]{:S(2)}) collective-permute-start(bf16[4,32,128]{2,1,0:T(8,128)(2,1)} %get-tuple-element.29), channel_id=1, source_target_pairs={{1,0},{2,1},{3,2},{4,3},{5,4},{6,5},{7,6},{8,7},{9,8},{10,9},{11,1... | collective-permute-start | bytes 98312 | tf_op jit(solution)/shard_map/ppermute | solution.py:26
  33.7 136.6 %collective-permute-start.3 = (bf16[4,32,128]{2,1,0:T(8,128)(2,1)}, bf16[4,32,128]{2,1,0:T(8,128)(2,1)}, u32[]{:S(2)}, u32[]{:S(2)}) collective-permute-start(bf16[4,32,128]{2,1,0:T(8,128)(2,1)} %get-tuple-element.28), channel_id=1, source_target_pairs={{0,1},{1,2},{2,3},{3,4},{4,5},{5,6},{6,7},{7,8},{8,9},{9,10},{10,1... | collective-permute-start | bytes 98312 | tf_op jit(solution)/shard_map/ppermute | solution.py:26
  38.8 2.4 %copy-start.11 = (s32[1,24]{1,0:T(1,128)S(1)}, s32[1,24]{1,0:T(1,128)}, u32[]{:S(2)}) copy-start(s32[1,24]{1,0:T(1,128)} %param.23) | copy-start | bytes 292
  39.5 2.4 %copy-start.12 = (pred[24]{0:T(512)(128)(4,1)}, pred[24]{0:T(512)(128)(4,1)S(1)}, u32[]{:S(2)}) copy-start(pred[24]{0:T(512)(128)(4,1)S(1)} %iota_compare_fusion.2) | copy-start | bytes 76
  40.2 2.7 %copy-start.8 = (f32[32,128,1]{1,0,2:T(8,128)}, f32[32,128,1]{1,0,2:T(8,128)S(1)}, u32[]{:S(2)}) copy-start(f32[32,128,1]{1,0,2:T(8,128)S(1)} %fusion.73) | copy-start | bytes 49156
  40.3 12.9 %copy-start.13 = (s32[32]{0:T(128)S(1)}, s32[32]{0:T(128)}, u32[]{:S(2)}) copy-start(s32[32]{0:T(128)} %param.20) | copy-start | bytes 388
  43.0 128.8 %all-to-all-start = ((f32[32,128,32]{1,2,0:T(8,128)}), f32[32,128,32]{1,2,0:T(8,128)}, u32[]{:S(2)}, u32[]{:S(2)}) async-start(f32[32,128,32]{1,2,0:T(8,128)} %copy.48), calls=%async_computation | async-start | bytes 1048576 | tf_op jit(solution)/shard_map/all_to_all | solution.py:98
  54.9 102.8 %collective-permute-start = (bf16[32,512]{1,0:T(8,128)(2,1)}, bf16[32,512]{1,0:T(8,128)(2,1)}, u32[]{:S(2)}, u32[]{:S(2)}) collective-permute-start(bf16[32,512]{1,0:T(8,128)(2,1)} %get-tuple-element.30), channel_id=1, source_target_pairs={{0,1},{1,2},{2,3},{3,4},{4,5},{5,6},{6,7},{7,8},{8,9},{9,10},{10,1... | collective-permute-start | bytes 98312 | tf_op jit(solution)/shard_map/ppermute | solution.py:17
  57.6 100.2 %collective-permute-start.1 = (bf16[32,512]{1,0:T(8,128)(2,1)}, bf16[32,512]{1,0:T(8,128)(2,1)}, u32[]{:S(2)}, u32[]{:S(2)}) collective-permute-start(bf16[32,512]{1,0:T(8,128)(2,1)} %get-tuple-element.31), channel_id=1, source_target_pairs={{1,0},{2,1},{3,2},{4,3},{5,4},{6,5},{7,6},{8,7},{9,8},{10,9},{11,1... | collective-permute-start | bytes 98312 | tf_op jit(solution)/shard_map/ppermute | solution.py:18
  64.0 0.6 copy-start.9
  150.0 2.8 %copy-start.5 = (f32[1,128,128]{2,1,0:T(8,128)S(1)}, f32[1,128,128]{2,1,0:T(8,128)}, u32[]{:S(2)}) copy-start(f32[1,128,128]{2,1,0:T(8,128)} %param.26) | copy-start | bytes 196612
  162.2 7.0 %copy-start.3 = (bf16[32,64,128]{2,1,0:T(8,128)(2,1)S(1)}, bf16[32,64,128]{2,1,0:T(8,128)(2,1)}, u32[]{:S(2)}) copy-start(bf16[32,64,128]{2,1,0:T(8,128)(2,1)} %param.21) | copy-start | bytes 1572868
  162.2 7.0 %copy-start.7 = (bf16[32,64,32]{1,2,0:T(8,128)(2,1)S(1)}, bf16[32,64,32]{1,2,0:T(8,128)(2,1)}, u32[]{:S(2)}) copy-start(bf16[32,64,32]{1,2,0:T(8,128)(2,1)} %fusion.18) | copy-start | bytes 393220
  169.2 3.7 %copy-start.6 = (f32[1,128,128]{2,1,0:T(8,128)S(1)}, f32[1,128,128]{2,1,0:T(8,128)}, u32[]{:S(2)}) copy-start(f32[1,128,128]{2,1,0:T(8,128)} %param.26) | copy-start | bytes 196612
  169.2 3.7 %copy-start.10 = (f32[128,32]{0,1:T(8,128)S(1)}, f32[128,32]{0,1:T(8,128)}, u32[]{:S(2)}) copy-start(f32[128,32]{0,1:T(8,128)} %convolution_bitcast_fusion.3) | copy-start | bytes 49156
  169.2 3.9 %copy-start.2 = (f32[32,64,128]{2,1,0:T(8,128)S(1)}, f32[32,64,128]{2,1,0:T(8,128)}, u32[]{:S(2)}) copy-start(f32[32,64,128]{2,1,0:T(8,128)} %param.22) | copy-start | bytes 3145732
where the time goes:
time: 180 us; the launch traced here: 178 us
  blocking collectives  80.6 us (45%)
  matrix products  37.8 us (21%)
  other arithmetic  30.6 us (17%)
  starting transfers between devices  19.1 us (11%)
  local copies, waits for them, and re-layouts  8.43 us (5%)
    all_gather x1, blocking collectives, shards(): lax.all_gather(parent_right[None], ('slab', 'leaf'), axis=0, tiled=True)  39 us
    psum x1, blocking collectives, shards(): within = lax.psum(slab_share, 'leaf')  31.6 us
    scatter-add x1, other arithmetic, shards(): jax.ops.segment_sum(contrib.reshape(-1, rhs_count, B), offsets.reshape(-1...  22.6 us
    all_to_all x1, starting transfers between devices, shards(): lax.all_to_all(spread, ('slab', 'leaf'), split_axis=0, concat_axis=0, til...  10.2 us
    all_gather x1, blocking collectives, shards(): slab_sum_totals = lax.all_gather(within[None], 'slab', axis=0, tiled=True)  9.96 us
    dot_general x1, matrix products, shards(): jnp.einsum('csab,rcsb->rca', near_blocks, picked, preferred_element_type=...  6.94 us
    dot_general x1, matrix products, shards(): jnp.einsum('csab,rca->csrb', near_blocks, masked_left, preferred_element_...  6.65 us
    ppermute x2, starting transfers between devices, passed_along(): return lax.ppermute(block, axis, route)  4.93 us
  transfers between devices with their start and end apart: 5, of which 0 were waited for; matrix products, arithmetic and copies ran while one was open for 21% of the time, Pallas kernels for 0%

commit v1 on v0

--- a/solution.py
+++ b/solution.py
@@ -5,6 +5,10 @@
 
 B = 128
 HW = 4
+
+
+def trails_answer(local_x):
+    return lax.all_gather(local_x, "leaf").sum(axis=0)
 
 
 def extended_2(value, sides, width):
@@ -104,7 +108,7 @@
             jnp.einsum("qt,qr->tr", lift, parent_left, precision=uppermost_level),
         ]
     )
-    within = lax.psum(slab_share, "leaf")
+    within = trails_answer(slab_share)
     slab_sum_totals = lax.all_gather(within[None], "slab", axis=0, tiled=True)
     remaining_slabs = (jnp.arange(slab_count, dtype=jnp.int32) != slab_index).astype(jnp.float32)
     row_block_list = lax.dynamic_index_in_dim(apex_coupling, slab_index, 0, keepdims=False)

time: 180 us -> 170 us (0.944)
  blocking collectives: 80.6 us -> 70 us
    psum x1 -> x0, blocking collectives: 31.6 us -> none  [shards(): within = lax.psum(slab_share, 'leaf')]
    all_gather x0 -> x1, blocking collectives: none -> 17.2 us  [trails_answer(): return lax.all_gather(local_x, 'leaf').sum(axis=0)]
    all_gather x1, blocking collectives: 9.96 us -> 12.6 us  [shards(): slab_sum_totals = lax.all_gather(within[None], 'slab', axis=0, tiled=True)]
  transfers between devices with their start and end apart: 5 -> 5, of which waited for: 0 -> 0; matrix products, arithmetic and copies ran while one was open for 21% -> 23% of each run, Pallas kernels for 0% -> 0%
where the time goes in v1:
time: 170 us; the launch traced here: 169 us
  blocking collectives  70 us (41%)
  matrix products  37.8 us (22%)
  other arithmetic  31.6 us (19%)
  starting transfers between devices  19.1 us (11%)
  local copies, waits for them, and re-layouts  8.43 us (5%)
  between operations  1.71 us (1%)
    all_gather x1, blocking collectives, shards(): lax.all_gather(parent_right[None], ('slab', 'leaf'), axis=0, tiled=True)  40.3 us
    scatter-add x1, other arithmetic, shards(): jax.ops.segment_sum(contrib.reshape(-1, rhs_count, B), offsets.reshape(-1...  22.6 us
    all_gather x1, blocking collectives, trails_answer(): return lax.all_gather(local_x, 'leaf').sum(axis=0)  17.2 us
    all_gather x1, blocking collectives, shards(): slab_sum_totals = lax.all_gather(within[None], 'slab', axis=0, tiled=True)  12.6 us
    all_to_all x1, starting transfers between devices, shards(): lax.all_to_all(spread, ('slab', 'leaf'), split_axis=0, concat_axis=0, til...  10.2 us
    dot_general x1, matrix products, shards(): jnp.einsum('csab,rcsb->rca', near_blocks, picked, preferred_element_type=...  6.94 us
    dot_general x1, matrix products, shards(): jnp.einsum('csab,rca->csrb', near_blocks, masked_left, preferred_element_...  6.65 us
    ppermute x2, starting transfers between devices, passed_along(): return lax.ppermute(block, axis, route)  4.93 us
  transfers between devices with their start and end apart: 5, of which 0 were waited for; matrix products, arithmetic and copies ran while one was open for 23% of the time, Pallas kernels for 0%

profile of v1, /device:TPU:0, one launch (start us, length us, event | category | flops | bytes accessed | tf_op | source)
XLA Modules:
  0.0 168.6 jit_solution(3837336940379929815)
XLA Ops:
  0.6 0.0 copy-start
  0.7 0.8 compare_and_fusion
  1.5 0.1 copy.45
  1.5 0.1 reshape.132
  1.6 0.7 iota_compare_fusion
  2.4 6.7 %fusion.31 = f32[32,32,8,128]{3,1,2,0:T(8,128)} fusion(bf16[32,8,128,128]{3,2,1,0:T(8,128)(2,1)} %param.18, pred[32,128]{1,0:T(8,128)(4,1)S(1)} %iota_compare_fusion, bf16[32,4096]{1,0:T(8,128)(2,1)} %param.17), kind=kOutput, calls=%fused_computation.45 | convolution fusion | flops 268566528 | bytes 12849152 | tf_op jit(solution)/shard_map/csab,rca->csrb/dot_general | solution.py:65
  9.0 0.1 broadcast_in_dim.78
  9.1 0.0 copy-start.4
  9.1 22.6 %scatter_fusion = f32[40,32,128]{2,1,0:T(8,128)S(1)} fusion(f32[40,32,128]{2,1,0:T(8,128)S(1)} %broadcast_in_dim.78, s32[256]{0:T(256)S(1)} %reshape.132, f32[256,32,128]{2,1,0:T(8,128)} %bitcast.168), kind=kCustom, calls=%fused_computation.1 | custom fusion | flops 1048576 | bytes 12583936 | tf_op jit(solution)/shard_map/scatter-add | solution.py:68
  31.7 0.0 copy-start.1
  31.7 0.1 convert.9
  31.8 0.6 fusion.70
  32.4 1.3 collective-permute-start.2
  33.7 3.7 %collective-permute-start.3 = (bf16[4,32,128]{2,1,0:T(8,128)(2,1)}, bf16[4,32,128]{2,1,0:T(8,128)(2,1)}, u32[]{:S(2)}, u32[]{:S(2)}) collective-permute-start(bf16[4,32,128]{2,1,0:T(8,128)(2,1)} %get-tuple-element.28), channel_id=1, source_target_pairs={{0,1},{1,2},{2,3},{3,4},{4,5},{5,6},{6,7},{7,8},{8,9},{9,10},{10,1... | collective-permute-start | bytes 98312 | tf_op jit(solution)/shard_map/ppermute | solution.py:30
  37.4 1.4 convolution_bitcast_fusion
  39.5 0.7 fusion.73
  40.2 0.0 copy-start.8
  40.3 0.0 copy-start.13
  40.3 0.9 fusion.15
  41.2 0.6 fusion.27
  41.9 1.1 copy.47
  43.0 10.2 %all-to-all-start = ((f32[32,128,32]{1,2,0:T(8,128)}), f32[32,128,32]{1,2,0:T(8,128)}, u32[]{:S(2)}, u32[]{:S(2)}) async-start(f32[32,128,32]{1,2,0:T(8,128)} %copy.47), calls=%async_computation | async-start | bytes 1048576 | tf_op jit(solution)/shard_map/all_to_all | solution.py:102
  53.2 0.1 lt.59
  53.3 1.0 broadcast_select_fusion
  54.3 0.6 fusion.71
  54.9 2.7 %collective-permute-start = (bf16[32,512]{1,0:T(8,128)(2,1)}, bf16[32,512]{1,0:T(8,128)(2,1)}, u32[]{:S(2)}, u32[]{:S(2)}) collective-permute-start(bf16[32,512]{1,0:T(8,128)(2,1)} %get-tuple-element.30), channel_id=1, source_target_pairs={{0,1},{1,2},{2,3},{3,4},{4,5},{5,6},{6,7},{7,8},{8,9},{9,10},{10,1... | collective-permute-start | bytes 98312 | tf_op jit(solution)/shard_map/ppermute | solution.py:21
  57.6 1.3 collective-permute-start.1
  58.9 2.3 %convolution_bitcast_fusion.1 = f32[32,64,32]{1,2,0:T(8,128)} fusion(bf16[32,64,128]{2,1,0:T(8,128)(2,1)} %param.21, pred[32,128]{1,0:T(8,128)(4,1)S(1)} %iota_compare_fusion, bf16[32,4096]{1,0:T(8,128)(2,1)} %param.16), kind=kOutput, calls=%fused_computation.12 | convolution fusion | flops 16908288 | bytes 1052672 | tf_op jit(solution)/shard_map/ckb,rcb->ckr/dot_general | solution.py:80
  61.2 1.0 convolution_bitcast_fusion.5
  62.2 1.8 %fusion.72 = f32[32,128,1]{1,0,2:T(8,128)S(1)} fusion(f32[32,64,32]{1,2,0:T(8,128)} %convolution_bitcast_fusion.1, f32[32,64,128]{2,1,0:T(8,128)S(1)} %copy-done.1), kind=kOutput, calls=%fused_computation.97 | convolution fusion | flops 100663296 | bytes 1327104 | tf_op jit(solution)/shard_map/ckq,ckr->qr/dot_general | solution.py:86
  64.0 0.0 copy-start.9
  64.0 0.6 copy-done.9
  64.6 1.0 convolution_bitcast_fusion.6
  65.6 17.2 %all-gather.1 = f32[16,128,32]{1,2,0:T(8,128)} all-gather(f32[2,128,32]{1,2,0:T(8,128)S(1)} %pad_maximum_fusion), channel_id=3, replica_groups=mesh['slab'=4,'leaf'=8] {'leaf'}, dimensions={0}, use_global_device_ids=true | all-gather | bytes 294912 | tf_op jit(solution)/shard_map/all_gather | solution.py:11
  82.8 1.6 reduce_sum.18
  84.4 12.6 %all-gather.2 = f32[8,128,32]{1,2,0:T(8,128)} all-gather(f32[2,128,32]{1,2,0:T(8,128)} %reduce_sum.18), channel_id=4, replica_groups=mesh['slab'=4,'leaf'=8] {'slab'}, dimensions={0}, use_global_device_ids=true | all-gather | bytes 163840 | tf_op jit(solution)/shard_map/all_gather | solution.py:112
  97.0 1.8 %convolution_bitcast_fusion.3 = f32[128,32]{0,1:T(8,128)} fusion(f32[4,4,128,128]{3,2,1,0:T(8,128)} %param.27, s32[]{:T(128)S(6)} %select_n.42, f32[4,2,128,32]{2,3,1,0:T(8,128)} %bitcast.175, f32[4]{0:T(128)S(1)} %compare_convert_fusion), kind=kOutput, calls=%fused_computation.28 | convolution fusion | flops 25182208 | bytes 344084 | tf_op jit(solution)/shard_map/s,sab,sar->br/dot_general | solution.py:123
  98.8 1.3 convolution_bitcast_fusion.4
  100.2 40.3 %all-gather = f32[4096,32]{0,1:T(8,128)S(1)} all-gather(f32[128,32]{0,1:T(8,128)} %bitcast.177), channel_id=2, replica_groups=mesh['slab'=4,'leaf'=8] {'slab','leaf'}, dimensions={0}, use_global_device_ids=true | all-gather | bytes 540672 | tf_op jit(solution)/shard_map/all_gather | solution.py:91
  140.5 0.1 copy.57
  140.6 1.0 fusion.58
  141.6 1.6 fusion.20
  143.3 0.2 fusion.25
  143.5 3.6 %fusion.18 = bf16[32,64,32]{1,2,0:T(8,128)(2,1)} fusion(f32[32,128,1]{1,0,2:T(8,128)S(1)} %fusion.25, f32[32,64,128]{2,1,0:T(8,128)S(1)} %copy-done.1), kind=kOutput, calls=%fused_computation.22 | convolution fusion | flops 100728832 | bytes 1196032 | tf_op jit(solution)/shard_map/ckq,qr->ckr/dot_general | solution.py:132
  147.1 0.1 copy.38
  147.2 0.1 reshape.124
  147.3 0.8 slice.86
  148.1 0.1 copy.37
  148.2 0.8 copy_bitcast_fusion.2
  149.0 2.2 %gather_fusion = bf16[256,32,128]{2,1,0:T(8,128)(2,1)} fusion(bf16[32,40,128]{2,0,1:T(8,128)(2,1)S(1)} %copy_bitcast_fusion.2, s32[1024]{0:T(1024)S(1)} %pad_clamp_fusion), kind=kCustom, calls=%fused_computation | custom fusion | bytes 4195328 | tf_op jit(solution)/shard_map/jit(_take)/gather | solution.py:63
  151.2 1.4 fusion.44
  152.6 6.9 %fusion.8 = f32[32,32,128]{2,1,0:T(8,128)S(1)} fusion(bf16[32,8,128,128]{3,2,1,0:T(8,128)(2,1)} %param.18, bf16[32,8,32,128]{3,2,1,0:T(8,128)(2,1)} %bitcast.169, pred[32,8]{1,0:T(8,128)(4,1)S(1)} %copy.37), kind=kOutput, calls=%fused_computation.10 | convolution fusion | flops 269484032 | bytes 11010304 | tf_op jit(solution)/shard_map/csab,rcsb->rca/dot_general | solution.py:64
  159.6 0.0 copy-done.3
  159.6 0.0 copy-start.6
  159.6 0.0 copy-start.2
  159.7 0.3 fusion.14
  159.9 0.8 copy.75
  160.8 1.5 fusion.43
  162.2 1.1 reduce_sum.19
  163.3 0.2 fusion.24
  163.5 0.0 copy-done.2
  163.6 2.9 %fusion.19 = bf16[32,64,32]{1,2,0:T(8,128)(2,1)S(1)} fusion(f32[128,32,1]{0,1,2:T(8,128)S(1)} %fusion.24, f32[32,64,128]{2,1,0:T(8,128)S(1)} %copy-done.2), kind=kOutput, calls=%fused_computation.23 | convolution fusion | flops 100728832 | bytes 1196032 | tf_op jit(solution)/shard_map/ckq,qr->ckr/dot_general | solution.py:135
  166.5 1.3 fusion.12
  167.8 0.8 copy.74
  (28 shorter events, 0.1 us)
Async XLA Ops:
  0.6 39.6 %copy-start = (f32[1,24,128,128]{3,2,1,0:T(8,128)S(1)}, f32[1,24,128,128]{3,2,1,0:T(8,128)}, u32[]{:S(2)}) copy-start(f32[1,24,128,128]{3,2,1,0:T(8,128)} %param.25) | copy-start | bytes 4718596
  9.1 28.3 %copy-start.4 = (bf16[32,4096]{1,0:T(8,128)(2,1)S(1)}, bf16[32,4096]{1,0:T(8,128)(2,1)}, u32[]{:S(2)}) copy-start(bf16[32,4096]{1,0:T(8,128)(2,1)} %param.17) | copy-start | bytes 786436
  31.7 7.8 %copy-start.1 = (f32[32,64,128]{2,1,0:T(8,128)S(1)}, f32[32,64,128]{2,1,0:T(8,128)}, u32[]{:S(2)}) copy-start(f32[32,64,128]{2,1,0:T(8,128)} %param.22) | copy-start | bytes 3145732
  32.4 118.8 %collective-permute-start.2 = (bf16[4,32,128]{2,1,0:T(8,128)(2,1)}, bf16[4,32,128]{2,1,0:T(8,128)(2,1)}, u32[]{:S(2)}, u32[]{:S(2)}) collective-permute-start(bf16[4,32,128]{2,1,0:T(8,128)(2,1)} %get-tuple-element.29), channel_id=1, source_target_pairs={{1,0},{2,1},{3,2},{4,3},{5,4},{6,5},{7,6},{8,7},{9,8},{10,9},{11,1... | collective-permute-start | bytes 98312 | tf_op jit(solution)/shard_map/ppermute | solution.py:30
  33.7 127.1 %collective-permute-start.3 = (bf16[4,32,128]{2,1,0:T(8,128)(2,1)}, bf16[4,32,128]{2,1,0:T(8,128)(2,1)}, u32[]{:S(2)}, u32[]{:S(2)}) collective-permute-start(bf16[4,32,128]{2,1,0:T(8,128)(2,1)} %get-tuple-element.28), channel_id=1, source_target_pairs={{0,1},{1,2},{2,3},{3,4},{4,5},{5,6},{6,7},{7,8},{8,9},{9,10},{10,1... | collective-permute-start | bytes 98312 | tf_op jit(solution)/shard_map/ppermute | solution.py:30
  38.8 2.4 %copy-start.11 = (s32[1,24]{1,0:T(1,128)S(1)}, s32[1,24]{1,0:T(1,128)}, u32[]{:S(2)}) copy-start(s32[1,24]{1,0:T(1,128)} %param.23) | copy-start | bytes 292
  39.5 2.4 %copy-start.12 = (pred[24]{0:T(512)(128)(4,1)}, pred[24]{0:T(512)(128)(4,1)S(1)}, u32[]{:S(2)}) copy-start(pred[24]{0:T(512)(128)(4,1)S(1)} %iota_compare_fusion.2) | copy-start | bytes 76
  40.2 2.7 %copy-start.8 = (f32[32,128,1]{1,0,2:T(8,128)}, f32[32,128,1]{1,0,2:T(8,128)S(1)}, u32[]{:S(2)}) copy-start(f32[32,128,1]{1,0,2:T(8,128)S(1)} %fusion.73) | copy-start | bytes 49156
  40.3 12.9 %copy-start.13 = (s32[32]{0:T(128)S(1)}, s32[32]{0:T(128)}, u32[]{:S(2)}) copy-start(s32[32]{0:T(128)} %param.20) | copy-start | bytes 388
  43.0 119.3 %all-to-all-start = ((f32[32,128,32]{1,2,0:T(8,128)}), f32[32,128,32]{1,2,0:T(8,128)}, u32[]{:S(2)}, u32[]{:S(2)}) async-start(f32[32,128,32]{1,2,0:T(8,128)} %copy.47), calls=%async_computation | async-start | bytes 1048576 | tf_op jit(solution)/shard_map/all_to_all | solution.py:102
  54.9 93.3 %collective-permute-start = (bf16[32,512]{1,0:T(8,128)(2,1)}, bf16[32,512]{1,0:T(8,128)(2,1)}, u32[]{:S(2)}, u32[]{:S(2)}) collective-permute-start(bf16[32,512]{1,0:T(8,128)(2,1)} %get-tuple-element.30), channel_id=1, source_target_pairs={{0,1},{1,2},{2,3},{3,4},{4,5},{5,6},{6,7},{7,8},{8,9},{9,10},{10,1... | collective-permute-start | bytes 98312 | tf_op jit(solution)/shard_map/ppermute | solution.py:21
  57.6 90.6 %collective-permute-start.1 = (bf16[32,512]{1,0:T(8,128)(2,1)}, bf16[32,512]{1,0:T(8,128)(2,1)}, u32[]{:S(2)}, u32[]{:S(2)}) collective-permute-start(bf16[32,512]{1,0:T(8,128)(2,1)} %get-tuple-element.31), channel_id=1, source_target_pairs={{1,0},{2,1},{3,2},{4,3},{5,4},{6,5},{7,6},{8,7},{9,8},{10,9},{11,1... | collective-permute-start | bytes 98312 | tf_op jit(solution)/shard_map/ppermute | solution.py:22
  64.0 0.6 copy-start.9
  140.5 2.8 %copy-start.5 = (f32[1,128,128]{2,1,0:T(8,128)S(1)}, f32[1,128,128]{2,1,0:T(8,128)}, u32[]{:S(2)}) copy-start(f32[1,128,128]{2,1,0:T(8,128)} %param.26) | copy-start | bytes 196612
  152.6 7.0 %copy-start.3 = (bf16[32,64,128]{2,1,0:T(8,128)(2,1)S(1)}, bf16[32,64,128]{2,1,0:T(8,128)(2,1)}, u32[]{:S(2)}) copy-start(bf16[32,64,128]{2,1,0:T(8,128)(2,1)} %param.21) | copy-start | bytes 1572868
  152.6 7.0 %copy-start.7 = (bf16[32,64,32]{1,2,0:T(8,128)(2,1)S(1)}, bf16[32,64,32]{1,2,0:T(8,128)(2,1)}, u32[]{:S(2)}) copy-start(bf16[32,64,32]{1,2,0:T(8,128)(2,1)} %fusion.18) | copy-start | bytes 393220
  159.6 3.7 %copy-start.6 = (f32[1,128,128]{2,1,0:T(8,128)S(1)}, f32[1,128,128]{2,1,0:T(8,128)}, u32[]{:S(2)}) copy-start(f32[1,128,128]{2,1,0:T(8,128)} %param.26) | copy-start | bytes 196612
  159.6 3.7 %copy-start.10 = (f32[128,32]{0,1:T(8,128)S(1)}, f32[128,32]{0,1:T(8,128)}, u32[]{:S(2)}) copy-start(f32[128,32]{0,1:T(8,128)} %convolution_bitcast_fusion.3) | copy-start | bytes 49156
  159.6 3.9 %copy-start.2 = (f32[32,64,128]{2,1,0:T(8,128)S(1)}, f32[32,64,128]{2,1,0:T(8,128)}, u32[]{:S(2)}) copy-start(f32[32,64,128]{2,1,0:T(8,128)} %param.22) | copy-start | bytes 3145732
